TPU v7x, 32 devices: a whole 2x2x4 slice. The times are simulated.
32 devices in a mesh: ent: 8 (over z, x), qry: 4 (over y, core).
Axes of the slice: x: 2, y: 2, z: 4, core: 2. Of those that a mesh axis runs over, the one named last changes fastest.
Arguments:
- ent_feat: bfloat16 [64, 8192], P(None, 'ent'), may hold values from -6 to 6
- query_head: int32 [16], replicated, may hold values from 0 to 8191
- query_rel: int32 [16], replicated, may hold values from 0 to 821
- query_table: bfloat16 [822, 64], replicated, may hold values from -5 to 5
- rel_table: bfloat16 [3, 822, 64], replicated, may hold values from -5 to 5
- layer_weight: bfloat16 [3, 64, 64], replicated, may hold values from -0.75 to 0.75
- layer_bias: float32 [3, 64], replicated, may hold values from -5 to 5
- norm_gain: float32 [3, 64], replicated, may hold values from 0.5 to 1.5
- norm_shift: float32 [3, 64], replicated, may hold values from -3 to 3
- reg_blocks: int32 [640, 2], P('ent'), may hold values from 0 to 63, as said below
- reg_rel: int32 [640], P('ent'), may hold values from 0 to 821
- reg_mask: int32 [640, 128, 128], P('ent'), may hold values 0 or 1
- hin_blocks: int32 [192, 2], P('ent'), may hold values from 0 to 63, as said below
- hin_rel: int32 [192], P('ent'), may hold values from 0 to 821
- hin_mask: int32 [192, 128, 128], P('ent'), may hold values 0 or 1
- hout_blocks: int32 [192, 2], P('ent'), may hold values from 0 to 63, as said below
- hout_rel: int32 [192], P('ent'), may hold values from 0 to 821
- hout_mask: int32 [192, 128, 128], P('ent'), may hold values 0 or 1
- read_weight: bfloat16 [128, 64], replicated, may hold values from -0.5 to 0.5
- read_bias: float32 [64], replicated, may hold values from -5 to 5
- read_out: float32 [64], replicated, may hold values from -0.75 to 0.75
Outputs:
- scores: float32 [16, 8192], P(None, ('ent', 'qry'))
- hub_scores: float32 [16, 128], P('qry', 'ent')
Inputs may be any that keep to these rules, and one draw needn't show every extreme that they name: `reg_blocks`: rows are grouped by 80 per index of ent. Column 0 is a block of that index's own 8 blocks; column 1 is a block of the same index's or an adjacent index's entities. `hin_blocks`: rows are grouped by 24 per index of ent. Column 0 is a hub block, below 1; column 1 is a block of that index's own entities. `hout_blocks`: rows are grouped by 24 per index of ent. Column 0 is a block of that index's own entities; column 1 is a hub block, below 1.
All inputs are finite; a program needn't handle non-finite values. No bound on the sum of `reg_mask` or of `hin_mask` or of `hout_mask` on one device may be relied on, other than what follows from the above.
Results may differ from a plain program's by a relative error of at most 0.0075.
Values may be sent and summed in bfloat16 or wider, within the bound.
No kernel may reach another device: no remote copies, remote signals or barrier semaphores. Data moves between devices by JAX's collectives and lax.ppermute only.
A program may use at most 128 MiB of HBM per device.

v0:
```python
import jax
import jax.numpy as jnp
from jax import lax
from jax.sharding import PartitionSpec as P

LAYERS = 3
HUB_DEV = 16


def padded(cells, sides, width):
    for axis, dim in sides:
        count = lax.axis_size(axis)
        ends = count - 1
        head = lax.slice_in_dim(cells, 0, width, axis=dim)
        tail = lax.slice_in_dim(cells, cells.shape[dim] - width, cells.shape[dim], axis=dim)
        cells = jnp.concatenate(
            [
                lax.ppermute(tail, axis, [(i, (i + 1) % count) for i in range(ends)]),
                cells,
                lax.ppermute(head, axis, [((i + 1) % count, i) for i in range(ends)]),
            ],
            axis=dim,
        )
    return cells


def normalize(values, along_axis, gain_rows, shift_rows):
    average = jnp.mean(values, axis=along_axis, keepdims=True)
    centered = values - average
    variance = jnp.mean(centered * centered, axis=along_axis, keepdims=True)
    return centered * lax.rsqrt(variance + 1e-05) * gain_rows + shift_rows


def update_hubs(hub_sum, hub_old, weight, bias_row, gain_row, shift_row, q_local, model_width):
    count = hub_sum.shape[0]
    inputs_now = hub_sum.astype(jnp.bfloat16).reshape(count, q_local, model_width)
    linear = (
        jnp.einsum("hqd,de->hqe", inputs_now, weight, preferred_element_type=jnp.float32)
        + bias_row[None, None, :]
    )
    normed = normalize(linear, 2, gain_row[None, None, :], shift_row[None, None, :])
    updated = jax.nn.relu(normed) + hub_old.astype(jnp.float32).reshape(count, q_local, model_width)
    return updated.astype(jnp.bfloat16).reshape(count, q_local * model_width)


def body(
    ent_feat,
    query_head,
    query_rel,
    query_table,
    rel_table,
    layer_weight,
    layer_bias,
    norm_gain,
    norm_shift,
    reg_blocks,
    reg_rel,
    reg_mask,
    hin_blocks,
    hin_rel,
    hin_mask,
    hout_blocks,
    hout_rel,
    hout_mask,
    read_weight,
    read_bias,
    read_out,
):
    ent_devices = lax.axis_size("ent")
    queries = query_head.shape[0]
    q_local = queries // lax.axis_size("qry")
    model_width = ent_feat.shape[0]
    ent_local = ent_feat.shape[1]
    block_size = reg_mask.shape[1]
    blocks_local = ent_local // block_size
    hub_total = HUB_DEV * ent_devices
    hub_block_count = hub_total // block_size
    state_rows = q_local * model_width
    first_block = lax.axis_index("ent") * blocks_local
    first_entity = lax.axis_index("ent") * ent_local
    query_first = lax.axis_index("qry") * q_local
    highest = lax.Precision.HIGHEST
    rel_iota = jnp.arange(query_table.shape[0], dtype=jnp.int32)
    query_onehot = (query_rel[:, None] == rel_iota[None, :]).astype(jnp.bfloat16)
    query_all = jnp.dot(query_onehot, query_table, preferred_element_type=jnp.float32)
    query_local = lax.dynamic_slice_in_dim(query_all, query_first, q_local, 0)
    heads_local = lax.dynamic_slice_in_dim(query_head, query_first, q_local, 0)
    positions = first_entity + jnp.arange(ent_local, dtype=jnp.int32)
    head_hits = (heads_local[:, None] == positions[None, :]).astype(jnp.float32)
    boundary = query_local[:, :, None] * head_hits[:, None, :]
    states = (ent_feat.astype(jnp.float32)[None] + boundary).astype(jnp.bfloat16)
    reg_masks = reg_mask.astype(jnp.bfloat16)
    hin_masks = hin_mask.astype(jnp.bfloat16)
    hout_masks = hout_mask.astype(jnp.bfloat16)
    local_iota = jnp.arange(blocks_local, dtype=jnp.int32)[None, :]
    reg_onehot = (reg_blocks[:, 0][:, None] - first_block == local_iota).astype(jnp.float32)
    reg_sources = reg_blocks[:, 1] - first_block + blocks_local
    hout_onehot = (hout_blocks[:, 0][:, None] - first_block == local_iota).astype(jnp.float32)
    hout_sources = hout_blocks[:, 1]
    hin_onehot = (
        hin_blocks[:, 0][:, None] == jnp.arange(hub_block_count, dtype=jnp.int32)[None, :]
    ).astype(jnp.float32)
    hin_sources = hin_blocks[:, 1] - first_block

    def tile_coefficients(rel_ids, rel_layer):
        rel_onehot = (rel_ids[:, None] == rel_iota[None, :]).astype(jnp.bfloat16)
        rel_rows = jnp.dot(rel_onehot, rel_layer, preferred_element_type=jnp.float32)
        return (query_local[:, :, None] * rel_rows.T[None, :, :]).reshape(state_rows, -1)

    hub_own = jnp.zeros((HUB_DEV, state_rows), jnp.bfloat16)
    for layer_at in range(LAYERS):
        weight = layer_weight[layer_at]
        rel_layer = rel_table[layer_at]
        flat_states = states.reshape(state_rows, ent_local)
        window = padded(flat_states, (("ent", 1),), ent_local)
        window_blocks = window.reshape(state_rows, 3 * blocks_local, block_size)
        gathered = jnp.take(window_blocks, reg_sources, axis=1)
        product = jnp.einsum(
            "ctj,tjk->ctk", gathered, reg_masks, preferred_element_type=jnp.float32
        )
        product = product * tile_coefficients(reg_rel, rel_layer)[:, :, None]
        totals = jnp.einsum("ctk,tb->cbk", product, reg_onehot, precision=highest)
        if layer_at > 0:
            hub_full = lax.all_gather(hub_own, "ent", axis=0, tiled=True)
        else:
            hub_full = jnp.zeros((hub_total, state_rows), jnp.bfloat16)
        hub_view = hub_full.reshape(hub_block_count, block_size, state_rows)
        hub_sources = jnp.take(hub_view, hout_sources, axis=0)
        product = jnp.einsum(
            "tjc,tjk->ctk", hub_sources, hout_masks, preferred_element_type=jnp.float32
        )
        product = product * tile_coefficients(hout_rel, rel_layer)[:, :, None]
        totals = totals + jnp.einsum("ctk,tb->cbk", product, hout_onehot, precision=highest)
        own_blocks = flat_states.reshape(state_rows, blocks_local, block_size)
        hin_gathered = jnp.take(own_blocks, hin_sources, axis=1)
        hin_product = jnp.einsum(
            "ctj,tjk->tkc", hin_gathered, hin_masks, preferred_element_type=jnp.float32
        )
        hin_product = hin_product * tile_coefficients(hin_rel, rel_layer).T[:, None, :]
        partial_value = jnp.einsum(
            "tkc,th->hkc", hin_product, hin_onehot, precision=highest
        ).reshape(hub_total, state_rows)
        inputs_now = (totals.reshape(q_local, model_width, ent_local) + boundary).astype(
            jnp.bfloat16
        )
        linear = (
            jnp.einsum("qdv,de->qev", inputs_now, weight, preferred_element_type=jnp.float32)
            + layer_bias[layer_at][None, :, None]
        )
        normed = normalize(
            linear, 1, norm_gain[layer_at][None, :, None], norm_shift[layer_at][None, :, None]
        )
        states = (jax.nn.relu(normed) + states.astype(jnp.float32)).astype(jnp.bfloat16)
        hub_sum = lax.psum_scatter(partial_value, "ent", scatter_dimension=0, tiled=True)
        hub_own = update_hubs(
            hub_sum,
            hub_own,
            weight,
            layer_bias[layer_at],
            norm_gain[layer_at],
            norm_shift[layer_at],
            q_local,
            model_width,
        )
    read_states = read_weight[:model_width]
    query_part_all = (
        jnp.dot(
            query_all.astype(jnp.bfloat16),
            read_weight[model_width:],
            preferred_element_type=jnp.float32,
        )
        + read_bias[None, :]
    )
    query_part_local = lax.dynamic_slice_in_dim(query_part_all, query_first, q_local, 0)
    moved_states = lax.all_to_all(states, "qry", split_axis=2, concat_axis=0, tiled=True)
    features = jax.nn.relu(
        jnp.einsum("qdv,de->qev", moved_states, read_states, preferred_element_type=jnp.float32)
        + query_part_all[:, :, None]
    )
    scores = jnp.einsum("qev,e->qv", features, read_out, precision=highest)
    hub_view_own = hub_own.reshape(HUB_DEV, q_local, model_width)
    hub_features = jax.nn.relu(
        jnp.einsum("hqd,de->hqe", hub_view_own, read_states, preferred_element_type=jnp.float32)
        + query_part_local[None]
    )
    hub_scores = jnp.einsum("hqe,e->qh", hub_features, read_out, precision=highest)
    return (scores, hub_scores)


def solution(mesh):
    return jax.shard_map(
        body,
        mesh=mesh,
        in_specs=(
            P(None, "ent"),
            P(),
            P(),
            P(),
            P(),
            P(),
            P(),
            P(),
            P(),
            P("ent", None),
            P("ent"),
            P("ent", None, None),
            P("ent", None),
            P("ent"),
            P("ent", None, None),
            P("ent", None),
            P("ent"),
            P("ent", None, None),
            P(),
            P(),
            P(),
        ),
        out_specs=(P(None, ("ent", "qry")), P("qry", "ent")),
        check_vma=False,
    )
```

profile of v0, /device:TPU:0, one launch (start us, length us, event | category | flops | bytes accessed | tf_op | source)
XLA Modules:
  0.0 461.3 jit_solution(1653198230750983543)
XLA Ops:
  12.1 1.3 collective-permute-start.1
  13.4 6.3 %collective-permute-start = (bf16[256,1024]{1,0:T(8,128)(2,1)}, bf16[256,1024]{1,0:T(8,128)(2,1)}, u32[]{:S(2)}, u32[]{:S(2)}) collective-permute-start(bf16[256,1024]{1,0:T(8,128)(2,1)} %fusion.90), channel_id=1, source_target_pairs={{0,4},{4,8},{8,12},{12,16},{16,20},{20,24},{24,28},{1,5},{5,9},{9,... | collective-permute-start | bytes 1572872 | tf_op jit(solution)/shard_map/ppermute | solution.py:18
  21.9 1.1 convolution_bitcast_fusion.5
  23.0 1.1 convolution_bitcast_fusion.6
  27.7 1.2 copy.242
  31.9 1.7 fusion.88
  34.5 2.0 gather_fusion.2
  36.5 1.4 multiply_bitcast_fusion.3
  37.9 4.0 multiply_bitcast_fusion.2
  41.9 3.6 copy.219
  45.5 3.2 fusion.172
  50.2 1.2 convolution_bitcast_fusion
  51.4 1.2 convolution_bitcast_fusion.1
  52.5 1.2 convolution_bitcast_fusion.2
  54.8 1.2 bitcast_multiply_fusion.5
  56.1 3.9 fusion.28
  64.0 48.3 %reduce-scatter.4.cloned.1.call-done = f32[16,256]{1,0:T(8,128)} async-done(((f32[128,256]{1,0:T(8,128)}), f32[16,256]{1,0:T(8,128)}) %reduce-scatter.4.cloned.1.call-update) | async-done | bytes 16400 | tf_op jit(solution)/shard_map/reduce_scatter | solution.py:154
  114.6 1.1 copy.243
  115.7 1.1 copy.240
  117.5 5.9 %gather_fusion = bf16[80,256,128]{2,1,0:T(8,128)(2,1)} fusion(bf16[256,24,128]{2,0,1:T(8,128)(2,1)S(1)} %copy.179, s32[1024]{0:T(1024)} %pad_clamp_fusion.1), kind=kCustom, calls=%fused_computation.clone | custom fusion | bytes 10486080 | tf_op jit(solution)/shard_map/jit(_take)/gather | solution.py:117
  123.5 6.6 %bitcast_multiply_fusion.2 = f32[256,80,128]{2,0,1:T(8,128)S(1)} fusion(f32[256,80]{0,1:T(8,128)S(1)} %copy-done.19, bf16[80,256,128]{2,1,0:T(8,128)(2,1)} %gather_fusion, pred[80]{0:T(512)(128)(4,1)S(1)} %copy-done.37, s32[80,128,128]{2,1,0:T(8,128)} %param.38), kind=kOutput, calls=%fused_computation.8 | convolution fusion | flops 677642240 | bytes 21053520 | tf_op jit(solution)/shard_map/ctj,tjk->ctk/dot_general | solution.py:118
  130.1 9.4 %fusion.78 = bf16[256,8,128]{2,1,0:T(8,128)(2,1)S(1)} fusion(f32[256,8,128]{2,1,0:T(8,128)S(1)} %get-tuple-element.12, f32[8,256,128]{2,0,1:T(8,128)S(1)} %copy-done.15, f32[256,80,128]{2,0,1:T(8,128)S(1)} %bitcast_multiply_fusion.2, s32[80]{0:T(128)S(1)} %copy-done.43), kind=kOutput, calls=%fused_computation.76 | convolution fusion | flops 252445312 | bytes 13107520 | tf_op jit(solution)/shard_map/ctk,tb->cbk/dot_general | solution.py:122
  141.8 1.1 add_convert_fusion.2
  143.8 2.1 gather_fusion.4
  145.9 4.4 multiply_bitcast_fusion.1
  150.3 3.6 copy.222
  153.9 3.2 fusion.170
  159.3 2.0 copy.184
  161.3 1.3 collective-permute-start.3
  162.6 5.4 %collective-permute-start.2 = (bf16[256,1024]{0,1:T(8,128)(2,1)}, bf16[256,1024]{0,1:T(8,128)(2,1)}, u32[]{:S(2)}, u32[]{:S(2)}) collective-permute-start(bf16[256,1024]{0,1:T(8,128)(2,1)} %copy.184), channel_id=1, source_target_pairs={{0,4},{4,8},{8,12},{12,16},{16,20},{20,24},{24,28},{1,5},{5,9},{9,... | collective-permute-start | bytes 1572872 | tf_op jit(solution)/shard_map/ppermute | solution.py:18
  168.0 52.6 %reduce-scatter.6.cloned.1.call-done = f32[16,256]{1,0:T(8,128)} async-done(((f32[128,256]{1,0:T(8,128)}), f32[16,256]{1,0:T(8,128)}) %reduce-scatter.6.cloned.1.call-update) | async-done | bytes 16400 | tf_op jit(solution)/shard_map/reduce_scatter | solution.py:154
  220.6 1.3 convert_element_type.125
  221.9 1.4 reshape.381
  224.4 1.4 add_convert_fusion.5
  226.0 32.4 %all_gather.6 = bf16[128,256]{1,0:T(8,128)(2,1)} all-gather(bf16[16,256]{1,0:T(8,128)(2,1)S(1)} %reshape.378), channel_id=1, replica_groups=mesh['ent'=8,'qry'=4] {'ent'}, dimensions={0}, use_global_device_ids=true | all-gather | bytes 73728 | tf_op jit(solution)/shard_map/all_gather | solution.py:124
  258.4 1.6 copy.195
  260.7 32.4 %all_gather.7 = bf16[128,256]{1,0:T(8,128)(2,1)} all-gather(bf16[16,256]{1,0:T(8,128)(2,1)S(1)} %reshape.382), channel_id=1, replica_groups=mesh['ent'=8,'qry'=4] {'ent'}, dimensions={0}, use_global_device_ids=true | all-gather | bytes 73728 | tf_op jit(solution)/shard_map/all_gather | solution.py:124
  293.1 1.6 copy.209
  294.7 1.8 bitcast_multiply_fusion.4
  296.5 3.8 fusion.26
  300.4 2.4 bitcast_multiply_fusion.3
  302.8 2.0 copy.188
  304.8 2.0 copy.186
  306.9 1.4 pad_maximum_fusion.1
  308.3 5.9 %gather_fusion.1 = bf16[80,256,128]{2,1,0:T(8,128)(2,1)} fusion(bf16[256,24,128]{2,0,1:T(8,128)(2,1)S(1)} %pad_maximum_fusion.1, s32[1024]{0:T(1024)} %pad_clamp_fusion.1), kind=kCustom, calls=%fused_computation.2.clone | custom fusion | bytes 10486080 | tf_op jit(solution)/shard_map/jit(_take)/gather | solution.py:117
  314.2 6.5 %bitcast_multiply_fusion.1 = f32[256,80,128]{2,0,1:T(8,128)S(1)} fusion(f32[256,80]{0,1:T(8,128)S(1)} %copy-done.18, bf16[80,256,128]{2,1,0:T(8,128)(2,1)} %gather_fusion.1, pred[80]{0:T(512)(128)(4,1)S(1)} %copy-done.38, s32[80,128,128]{2,1,0:T(8,128)} %param.38), kind=kOutput, calls=%fused_computation.7 | convolution fusion | flops 677642240 | bytes 21053520 | tf_op jit(solution)/shard_map/ctj,tjk->ctk/dot_general | solution.py:118
  320.8 9.4 %fusion.81 = bf16[256,8,128]{2,1,0:T(8,128)(2,1)S(1)} fusion(f32[256,8,128]{2,1,0:T(8,128)S(1)} %get-tuple-element.12, f32[8,256,128]{2,0,1:T(8,128)S(1)} %copy-done.17, f32[256,80,128]{2,0,1:T(8,128)S(1)} %bitcast_multiply_fusion.1, s32[80]{0:T(128)S(1)} %copy-done.44), kind=kOutput, calls=%fused_computation.77 | convolution fusion | flops 252445312 | bytes 13107520 | tf_op jit(solution)/shard_map/ctk,tb->cbk/dot_general | solution.py:122
  330.4 1.1 fusion.199
  331.8 1.4 add_convert_fusion.1
  334.1 2.1 gather_fusion.5
  336.2 4.2 multiply_bitcast_fusion
  340.4 3.6 copy.226
  343.9 3.2 fusion.168
  347.8 5.7 %fusion.24 = f32[8,256,128]{2,0,1:T(8,128)} fusion(f32[256,24,128]{2,0,1:T(8,128)} %bitcast_multiply_fusion.3, s32[24]{0:T(128)S(1)} %copy-done.48), kind=kOutput, calls=%fused_computation.30 | convolution fusion | flops 75497664 | bytes 4194400 | tf_op jit(solution)/shard_map/ctk,tb->cbk/dot_general | solution.py:133
  353.7 1.3 collective-permute-start.5
  355.0 4.6 collective-permute-start.4
  359.6 49.5 %reduce-scatter.8.cloned.1.call-done = f32[16,256]{1,0:T(8,128)} async-done(((f32[128,256]{1,0:T(8,128)}), f32[16,256]{1,0:T(8,128)}) %reduce-scatter.8.cloned.1.call-update) | async-done | bytes 16400 | tf_op jit(solution)/shard_map/reduce_scatter | solution.py:154
  412.3 1.4 pad_maximum_fusion.2
  413.7 5.8 %gather_fusion.3 = bf16[80,256,128]{2,1,0:T(8,128)(2,1)} fusion(bf16[256,24,128]{2,0,1:T(8,128)(2,1)S(1)} %pad_maximum_fusion.2, s32[1024]{0:T(1024)} %pad_clamp_fusion.1), kind=kCustom, calls=%fused_computation.3.clone | custom fusion | bytes 10486080 | tf_op jit(solution)/shard_map/jit(_take)/gather | solution.py:117
  419.5 6.6 %bitcast_multiply_fusion = f32[256,80,128]{2,0,1:T(8,128)S(1)} fusion(f32[256,80]{0,1:T(8,128)S(1)} %copy.203, bf16[80,256,128]{2,1,0:T(8,128)(2,1)} %gather_fusion.3, pred[80]{0:T(512)(128)(4,1)S(1)} %copy-done.38, s32[80,128,128]{2,1,0:T(8,128)} %param.38), kind=kOutput, calls=%fused_computation.6 | convolution fusion | flops 677642240 | bytes 21053520 | tf_op jit(solution)/shard_map/ctj,tjk->ctk/dot_general | solution.py:118
  426.1 9.4 %fusion.84 = bf16[256,8,128]{2,1,0:T(8,128)(2,1)S(1)} fusion(f32[256,8,128]{2,1,0:T(8,128)S(1)} %get-tuple-element.12, f32[8,256,128]{2,0,1:T(8,128)S(1)} %copy-done.16, f32[256,80,128]{2,0,1:T(8,128)S(1)} %bitcast_multiply_fusion, s32[80]{0:T(128)S(1)} %copy-done.45), kind=kOutput, calls=%fused_computation.78 | convolution fusion | flops 252445312 | bytes 13107520 | tf_op jit(solution)/shard_map/ctk,tb->cbk/dot_general | solution.py:122
  437.7 1.5 reshape.477
  439.2 3.5 all-to-all-start
  443.9 7.6 %all-to-all-done = bf16[4,2,32768]{2,1,0:T(2,128)(2,1)S(1)} async-done(((bf16[4,2,32768]{2,1,0:T(2,128)(2,1)}), bf16[4,2,32768]{2,1,0:T(2,128)(2,1)S(1)}, u32[]{:S(2)}, u32[]{:S(2)}) %all-to-all-start) | async-done | bytes 524320 | tf_op jit(solution)/shard_map/all_to_all | solution.py:175
  (238 shorter events, 42.7 us)
Async XLA Ops:
  7.2 105.1 %reduce-scatter.4.cloned.1.call-start = ((), (), s32[]{:S(2)}) async-start(), calls=%async_computation.4 | async-start | bytes 147456 | tf_op jit(solution)/shard_map/reduce_scatter | solution.py:154
  12.1 102.5 %collective-permute-start.1 = (bf16[256,1024]{1,0:T(8,128)(2,1)}, bf16[256,1024]{1,0:T(8,128)(2,1)}, u32[]{:S(2)}, u32[]{:S(2)}) collective-permute-start(bf16[256,1024]{1,0:T(8,128)(2,1)} %fusion.90), channel_id=1, source_target_pairs={{4,0},{8,4},{12,8},{16,12},{20,16},{24,20},{28,24},{5,1},{9,5},{13... | collective-permute-start | bytes 1572872 | tf_op jit(solution)/shard_map/ppermute | solution.py:20
  13.4 102.4 %collective-permute-start = (bf16[256,1024]{1,0:T(8,128)(2,1)}, bf16[256,1024]{1,0:T(8,128)(2,1)}, u32[]{:S(2)}, u32[]{:S(2)}) collective-permute-start(bf16[256,1024]{1,0:T(8,128)(2,1)} %fusion.90), channel_id=1, source_target_pairs={{0,4},{4,8},{8,12},{12,16},{16,20},{20,24},{24,28},{1,5},{5,9},{9,... | collective-permute-start | bytes 1572872 | tf_op jit(solution)/shard_map/ppermute | solution.py:18
  27.4 4.0 copy-start.35
  31.9 2.6 copy-start.42
  33.6 4.3 copy-start.6
  45.5 4.2 copy-start.62
  45.5 4.7 %copy-start.63 = (s32[80]{0:T(128)S(1)}, s32[80]{0:T(128)}, u32[]{:S(2)}) copy-start(s32[80]{0:T(128)} %param.37) | copy-start | bytes 964
  45.5 8.2 %copy-start.57 = (f32[3,64]{1,0:T(4,128)S(1)}, f32[3,64]{1,0:T(4,128)}, u32[]{:S(2)}) copy-start(f32[3,64]{1,0:T(4,128)} %param.33) | copy-start | bytes 2308
  45.5 8.8 %copy-start.61 = (s32[80,2]{0,1:T(2,128)S(1)}, s32[80,2]{0,1:T(2,128)}, u32[]{:S(2)}) copy-start(s32[80,2]{0,1:T(2,128)} %param.36) | copy-start | bytes 1924
  45.5 9.2 %copy-start.4 = (s32[24,128,128]{2,1,0:T(8,128)S(1)}, s32[24,128,128]{2,1,0:T(8,128)}, u32[]{:S(2)}) copy-start(s32[24,128,128]{2,1,0:T(8,128)} %param.44) | copy-start | bytes 4718596
  49.4 171.2 %reduce-scatter.6.cloned.1.call-start = ((), (), s32[]{:S(2)}) async-start(), calls=%async_computation.5 | async-start | bytes 147456 | tf_op jit(solution)/shard_map/reduce_scatter | solution.py:154
  50.2 9.7 %copy-start.46 = (s32[24]{0:T(128)}, s32[24]{0:T(128)S(1)}, u32[]{:S(2)}) copy-start(s32[24]{0:T(128)S(1)} %subtract_bitcast_fusion) | copy-start | bytes 292
  54.3 58.8 %copy-start.50 = (f32[64]{0:T(128)}, f32[64]{0:T(128)S(1)}, u32[]{:S(2)}) copy-start(f32[64]{0:T(128)S(1)} %get-tuple-element.22) | copy-start | bytes 772
  56.0 3.9 copy-start.58
  56.0 3.9 copy-start.59
  56.0 4.5 copy-start.26
  56.0 4.5 copy-start.34
  56.0 4.5 copy-start.60
  56.0 60.8 %copy-start.14 = (bf16[256,8,128]{2,1,0:T(8,128)(2,1)S(1)}, bf16[256,8,128]{2,1,0:T(8,128)(2,1)}, u32[]{:S(2)}) copy-start(bf16[256,8,128]{2,1,0:T(8,128)(2,1)} %copy-done.13) | copy-start | bytes 1572868
  60.7 51.6 %copy-start.29 = (f32[16,64]{1,0:T(8,128)}, f32[16,64]{1,0:T(8,128)S(1)}, u32[]{:S(2)}) copy-start(f32[16,64]{1,0:T(8,128)S(1)} %convolution_add_fusion.8) | copy-start | bytes 12292
  117.5 6.0 %copy-start.19 = (f32[256,80]{0,1:T(8,128)S(1)}, f32[256,80]{0,1:T(8,128)}, u32[]{:S(2)}) copy-start(f32[256,80]{0,1:T(8,128)} %copy.180) | copy-start | bytes 245764
  117.5 5.9 %copy-start.37 = (pred[80]{0:T(512)(128)(4,1)S(1)}, pred[80]{0:T(512)(128)(4,1)}, u32[]{:S(2)}) copy-start(pred[80]{0:T(512)(128)(4,1)} %get-tuple-element.9) | copy-start | bytes 244
  123.5 6.7 %copy-start.15 = (f32[8,256,128]{2,0,1:T(8,128)S(1)}, f32[8,256,128]{2,0,1:T(8,128)}, u32[]{:S(2)}) copy-start(f32[8,256,128]{2,0,1:T(8,128)} %fusion.28) | copy-start | bytes 3145732
  123.5 6.7 %copy-start.43 = (s32[80]{0:T(128)S(1)}, s32[80]{0:T(128)}, u32[]{:S(2)}) copy-start(s32[80]{0:T(128)} %subtract_bitcast_fusion.1) | copy-start | bytes 964
  130.1 9.6 %copy-start.51 = (f32[64]{0:T(128)S(1)}, f32[64]{0:T(128)}, u32[]{:S(2)}) copy-start(f32[64]{0:T(128)} %copy-done.50) | copy-start | bytes 772
  141.0 2.0 copy-start.22
  141.8 4.1 copy-start.7
  153.9 140.8 %copy-start.5 = (s32[24,128,128]{2,1,0:T(8,128)S(1)}, s32[24,128,128]{2,1,0:T(8,128)}, u32[]{:S(2)}) copy-start(s32[24,128,128]{2,1,0:T(8,128)} %param.44) | copy-start | bytes 4718596
  157.8 251.2 %reduce-scatter.8.cloned.1.call-start = ((), (), s32[]{:S(2)}) async-start(), calls=%async_computation.6 | async-start | bytes 147456 | tf_op jit(solution)/shard_map/reduce_scatter | solution.py:154
  161.3 141.4 %collective-permute-start.3 = (bf16[256,1024]{0,1:T(8,128)(2,1)}, bf16[256,1024]{0,1:T(8,128)(2,1)}, u32[]{:S(2)}, u32[]{:S(2)}) collective-permute-start(bf16[256,1024]{0,1:T(8,128)(2,1)} %copy.184), channel_id=1, source_target_pairs={{4,0},{8,4},{12,8},{16,12},{20,16},{24,20},{28,24},{5,1},{9,5},{13... | collective-permute-start | bytes 1572872 | tf_op jit(solution)/shard_map/ppermute | solution.py:20
  162.6 142.2 %collective-permute-start.2 = (bf16[256,1024]{0,1:T(8,128)(2,1)}, bf16[256,1024]{0,1:T(8,128)(2,1)}, u32[]{:S(2)}, u32[]{:S(2)}) collective-permute-start(bf16[256,1024]{0,1:T(8,128)(2,1)} %copy.184), channel_id=1, source_target_pairs={{0,4},{4,8},{8,12},{12,16},{16,20},{20,24},{24,28},{1,5},{5,9},{9,... | collective-permute-start | bytes 1572872 | tf_op jit(solution)/shard_map/ppermute | solution.py:18
  225.9 70.6 %copy-start.47 = (s32[24]{0:T(128)S(1)}, s32[24]{0:T(128)}, u32[]{:S(2)}) copy-start(s32[24]{0:T(128)} %copy-done.46) | copy-start | bytes 292
  296.5 3.9 copy-start.20
  296.5 3.9 copy-start.25
  296.5 3.8 copy-start.53
  308.2 6.0 %copy-start.18 = (f32[256,80]{0,1:T(8,128)S(1)}, f32[256,80]{0,1:T(8,128)}, u32[]{:S(2)}) copy-start(f32[256,80]{0,1:T(8,128)} %copy.189) | copy-start | bytes 245764
  308.2 5.9 %copy-start.38 = (pred[80]{0:T(512)(128)(4,1)S(1)}, pred[80]{0:T(512)(128)(4,1)}, u32[]{:S(2)}) copy-start(pred[80]{0:T(512)(128)(4,1)} %get-tuple-element.9) | copy-start | bytes 244
  314.2 6.6 %copy-start.17 = (f32[8,256,128]{2,0,1:T(8,128)S(1)}, f32[8,256,128]{2,0,1:T(8,128)}, u32[]{:S(2)}) copy-start(f32[8,256,128]{2,0,1:T(8,128)} %fusion.26) | copy-start | bytes 3145732
  314.2 6.6 %copy-start.44 = (s32[80]{0:T(128)S(1)}, s32[80]{0:T(128)}, u32[]{:S(2)}) copy-start(s32[80]{0:T(128)} %subtract_bitcast_fusion.1) | copy-start | bytes 964
  330.2 1.6 copy-start.3
  330.2 1.6 copy-start.23
  330.2 1.6 copy-start.32
  330.2 1.6 copy-start.40
  330.2 1.6 copy-start.41
  333.2 3.0 copy-start.8
  333.2 2.9 copy-start.24
  333.2 2.9 copy-start.39
  340.4 3.6 copy-start.36
  343.9 3.9 copy-start.48
  343.9 9.5 %copy-start.10 = (bf16[4,64,1024]{2,1,0:T(8,128)(2,1)S(1)}, bf16[4,64,1024]{2,1,0:T(8,128)(2,1)}, u32[]{:S(2)}) copy-start(bf16[4,64,1024]{2,1,0:T(8,128)(2,1)} %copy-done.9) | copy-start | bytes 1572868
  347.1 62.8 %copy-start.21 = (bf16[3,64,64]{2,1,0:T(8,128)(2,1)S(1)}, bf16[3,64,64]{2,1,0:T(8,128)(2,1)}, u32[]{:S(2)}) copy-start(bf16[3,64,64]{2,1,0:T(8,128)(2,1)} %param.32) | copy-start | bytes 73732
  347.1 62.8 %copy-start.49 = (f32[64]{0:T(128)S(1)}, f32[64]{0:T(128)}, u32[]{:S(2)}) copy-start(f32[64]{0:T(128)} %get-tuple-element.21) | copy-start | bytes 772
  353.7 56.6 %collective-permute-start.5 = (bf16[256,1024]{0,1:T(8,128)(2,1)S(1)}, bf16[256,1024]{0,1:T(8,128)(2,1)S(1)}, u32[]{:S(2)}, u32[]{:S(2)}) collective-permute-start(bf16[256,1024]{0,1:T(8,128)(2,1)S(1)} %copy.198), channel_id=1, source_target_pairs={{4,0},{8,4},{12,8},{16,12},{20,16},{24,20},{28,24},{5,1},{9,5},{13... | collective-permute-start | bytes 1572872 | tf_op jit(solution)/shard_map/ppermute | solution.py:20
  355.0 56.3 %collective-permute-start.4 = (bf16[256,1024]{0,1:T(8,128)(2,1)S(1)}, bf16[256,1024]{0,1:T(8,128)(2,1)S(1)}, u32[]{:S(2)}, u32[]{:S(2)}) collective-permute-start(bf16[256,1024]{0,1:T(8,128)(2,1)S(1)} %copy.198), channel_id=1, source_target_pairs={{0,4},{4,8},{8,12},{12,16},{16,20},{20,24},{24,28},{1,5},{5,9},{9,... | collective-permute-start | bytes 1572872 | tf_op jit(solution)/shard_map/ppermute | solution.py:18
  419.5 6.6 %copy-start.16 = (f32[8,256,128]{2,0,1:T(8,128)S(1)}, f32[8,256,128]{2,0,1:T(8,128)}, u32[]{:S(2)}) copy-start(f32[8,256,128]{2,0,1:T(8,128)} %fusion.24) | copy-start | bytes 3145732
  419.5 6.6 %copy-start.45 = (s32[80]{0:T(128)S(1)}, s32[80]{0:T(128)}, u32[]{:S(2)}) copy-start(s32[80]{0:T(128)} %subtract_bitcast_fusion.1) | copy-start | bytes 964
  436.6 6.1 %copy-start.27 = (bf16[128,64]{0,1:T(8,128)(2,1)S(1)}, bf16[128,64]{0,1:T(8,128)(2,1)}, u32[]{:S(2)}) copy-start(bf16[128,64]{0,1:T(8,128)(2,1)} %param.45) | copy-start | bytes 49156
  436.6 6.1 %copy-start.28 = (bf16[16,4,64]{2,0,1:T(8,128)(2,1)S(1)}, bf16[16,4,64]{2,0,1:T(8,128)(2,1)}, u32[]{:S(2)}) copy-start(bf16[16,4,64]{2,0,1:T(8,128)(2,1)} %get-tuple-element.4) | copy-start | bytes 24580
  436.6 6.1 %copy-start.54 = (f32[4,64]{1,0:T(4,128)S(1)}, f32[4,64]{1,0:T(4,128)}, u32[]{:S(2)}) copy-start(f32[4,64]{1,0:T(4,128)} %constant_dynamic-slice_fusion) | copy-start | bytes 3076
  436.6 6.4 %copy-start.52 = (f32[64]{0:T(128)S(1)}, f32[64]{0:T(128)}, u32[]{:S(2)}) copy-start(f32[64]{0:T(128)} %param.47) | copy-start | bytes 772
  437.6 15.1 %copy-start.30 = (f32[16,64]{1,0:T(8,128)S(1)}, f32[16,64]{1,0:T(8,128)}, u32[]{:S(2)}) copy-start(f32[16,64]{1,0:T(8,128)} %copy-done.29) | copy-start | bytes 12292
  439.2 12.3 %all-to-all-start = ((bf16[4,2,32768]{2,1,0:T(2,128)(2,1)}), bf16[4,2,32768]{2,1,0:T(2,128)(2,1)S(1)}, u32[]{:S(2)}, u32[]{:S(2)}) async-start(bf16[4,2,32768]{2,1,0:T(2,128)(2,1)} %reshape.477), calls=%async_computation.2 | async-start | bytes 1048576 | tf_op jit(solution)/shard_map/all_to_all | solution.py:175
  442.7 11.6 %copy-start.1 = (bf16[822,64]{0,1:T(8,128)(2,1)S(1)}, bf16[822,64]{0,1:T(8,128)(2,1)}, u32[]{:S(2)}) copy-start(bf16[822,64]{0,1:T(8,128)(2,1)} %param.30) | copy-start | bytes 315652
  (10 other events, 8.6 us)
Sparse Core Ops, SparseCore 0:
  49.6 62.6 reduce-scatter.3
  158.0 62.5 reduce-scatter.5
  347.9 61.0 reduce-scatter.7
where the time goes:
time: 468 us; the launch traced here: 461 us
  waiting for transfers between devices  158 us (34%)
  matrix products  107 us (23%)
  local copies, waits for them, and re-layouts  71.9 us (15%)
  blocking collectives  64.8 us (14%)
  starting transfers between devices  23.9 us (5%)
  other arithmetic  20.6 us (4%)
  between operations  15.3 us (3%)
    reduce_scatter x3, waiting for transfers between devices, body(): lax.psum_scatter(partial_value, 'ent', scatter_dimension=0, tiled=True)  150 us
    all_gather x2, blocking collectives, body(): hub_full = lax.all_gather(hub_own, 'ent', axis=0, tiled=True)  64.8 us
    dot_general x3, matrix products, body(): totals = jnp.einsum('ctk,tb->cbk', product, reg_onehot, precision=highest)  28.1 us
    dot_general x3, matrix products, body(): jnp.einsum('ctj,tjk->ctk', gathered, reg_masks, preferred_element_type=jn...  19.8 us
    gather x3, local copies, waits for them, and re-layouts, body(): gathered = jnp.take(window_blocks, reg_sources, axis=1)  17.7 us
    ppermute x3, starting transfers between devices, padded(): lax.ppermute(tail, axis, [(i, (i + 1) % count) for i in range(ends)])  16.3 us
    dot_general x3, matrix products, body(): jnp.einsum('ctk,tb->cbk', product, hout_onehot, precision=highest)  13.3 us
    dot_general x3, matrix products, body(): jnp.einsum('ctj,tjk->tkc', hin_gathered, hin_masks, preferred_element_typ...  12.6 us
  transfers between devices with their start and end apart: 10, of which 4 were waited for; matrix products, arithmetic and copies ran while one was open for 17% of the time, Pallas kernels for 0%

commit v1 on v0

--- a/solution.py
+++ b/solution.py
@@ -5,6 +5,27 @@
 
 LAYERS = 3
 HUB_DEV = 16
+
+
+def collect(x, axis, dim):
+    size, index, rows = (lax.axis_size(axis), lax.axis_index(axis), x.shape[dim])
+    right = [(i, (i + 1) % size) for i in range(size)]
+    backward = [(i, (i - 1) % size) for i in range(size)]
+    out = jnp.zeros((*x.shape[:dim], size * rows, *x.shape[dim + 1 :]), x.dtype)
+    out = lax.dynamic_update_slice_in_dim(out, x, index * rows, axis=dim)
+    from_left = from_right = x
+    halfway = size // 2
+    for step in range(1, halfway + 1):
+        from_left = lax.ppermute(from_left, axis, right)
+        out = lax.dynamic_update_slice_in_dim(
+            out, from_left, (index - step) % size * rows, axis=dim
+        )
+        if step < size - halfway:
+            from_right = lax.ppermute(from_right, axis, backward)
+            out = lax.dynamic_update_slice_in_dim(
+                out, from_right, (index + step) % size * rows, axis=dim
+            )
+    return out
 
 
 def padded(cells, sides, width):
@@ -121,7 +142,7 @@
         product = product * tile_coefficients(reg_rel, rel_layer)[:, :, None]
         totals = jnp.einsum("ctk,tb->cbk", product, reg_onehot, precision=highest)
         if layer_at > 0:
-            hub_full = lax.all_gather(hub_own, "ent", axis=0, tiled=True)
+            hub_full = collect(hub_own, "ent", 0)
         else:
             hub_full = jnp.zeros((hub_total, state_rows), jnp.bfloat16)
         hub_view = hub_full.reshape(hub_block_count, block_size, state_rows)

time: 468 us -> 450 us (0.962)
  blocking collectives: 64.8 us -> 0 us
  starting transfers between devices: 23.9 us -> 52.5 us
  local copies, waits for them, and re-layouts: 71.9 us -> 85.5 us
  waiting for transfers between devices: 158 us -> 163 us
    all_gather x2 -> x0, blocking collectives: 64.8 us -> none  [body(): hub_full = lax.all_gather(hub_own, 'ent', axis=0, tiled=True)]
    ppermute x0 -> x14, starting transfers between devices: none -> 28.3 us  [the longest x6 26.9 us: collect(): from_right = lax.ppermute(from_right, axis, backward)]
    dynamic_update_slice x0 -> x16, local copies, waits for them, and re-layouts: none -> 10.9 us  [the longest x8 5.43 us: collect(): lax.dynamic_update_slice_in_dim(out, from_left, (index - step) % size * r...]
    ppermute x0 -> x14, waiting for transfers between devices: none -> 5.02 us  [the longest x8 5 us: collect(): from_left = lax.ppermute(from_left, axis, right)]
  transfers between devices with their start and end apart: 10 -> 24, of which waited for: 4 -> 6; matrix products, arithmetic and copies ran while one was open for 17% -> 21% of each run, Pallas kernels for 0% -> 0%
where the time goes in v1:
time: 450 us; the launch traced here: 444 us
  waiting for transfers between devices  163 us (36%)
  matrix products  107 us (24%)
  local copies, waits for them, and re-layouts  85.5 us (19%)
  starting transfers between devices  52.5 us (12%)
  other arithmetic  20.7 us (5%)
  between operations  15.4 us (3%)
    reduce_scatter x3, waiting for transfers between devices, body(): lax.psum_scatter(partial_value, 'ent', scatter_dimension=0, tiled=True)  150 us
    dot_general x3, matrix products, body(): totals = jnp.einsum('ctk,tb->cbk', product, reg_onehot, precision=highest)  28.1 us
    ppermute x6, starting transfers between devices, collect(): from_right = lax.ppermute(from_right, axis, backward)  26.9 us
    dot_general x3, matrix products, body(): jnp.einsum('ctj,tjk->ctk', gathered, reg_masks, preferred_element_type=jn...  19.7 us
    gather x3, local copies, waits for them, and re-layouts, body(): gathered = jnp.take(window_blocks, reg_sources, axis=1)  17.6 us
    ppermute x3, starting transfers between devices, padded(): lax.ppermute(tail, axis, [(i, (i + 1) % count) for i in range(ends)])  16.3 us
    dot_general x3, matrix products, body(): jnp.einsum('ctk,tb->cbk', product, hout_onehot, precision=highest)  13.4 us
    dot_general x3, matrix products, body(): jnp.einsum('ctj,tjk->tkc', hin_gathered, hin_masks, preferred_element_typ...  12.6 us
  transfers between devices with their start and end apart: 24, of which 6 were waited for; matrix products, arithmetic and copies ran while one was open for 21% of the time, Pallas kernels for 0%

profile of v1, /device:TPU:0, one launch (start us, length us, event | category | flops | bytes accessed | tf_op | source)
XLA Modules:
  0.0 443.5 jit_solution(18056895279808356756)
XLA Ops:
  12.1 1.3 collective-permute-start.1
  13.3 6.3 %collective-permute-start = (bf16[256,1024]{1,0:T(8,128)(2,1)}, bf16[256,1024]{1,0:T(8,128)(2,1)}, u32[]{:S(2)}, u32[]{:S(2)}) collective-permute-start(bf16[256,1024]{1,0:T(8,128)(2,1)} %fusion.90), channel_id=1, source_target_pairs={{0,4},{4,8},{8,12},{12,16},{16,20},{20,24},{24,28},{1,5},{5,9},{9,... | collective-permute-start | bytes 1572872 | tf_op jit(solution)/shard_map/ppermute | solution.py:39
  27.8 1.2 copy.253
  32.0 1.7 fusion.88
  34.6 2.0 gather_fusion.2
  36.6 1.4 multiply_bitcast_fusion.3
  38.1 4.0 multiply_bitcast_fusion.2
  42.0 3.5 copy.230
  45.6 3.2 fusion.172
  51.7 1.2 convolution_bitcast_fusion.1
  55.2 1.2 bitcast_multiply_fusion.5
  56.5 3.9 fusion.28
  64.5 47.9 %reduce-scatter.4.cloned.1.call-done = f32[16,256]{1,0:T(8,128)} async-done(((f32[128,256]{1,0:T(8,128)}), f32[16,256]{1,0:T(8,128)}) %reduce-scatter.4.cloned.1.call-update) | async-done | bytes 16400 | tf_op jit(solution)/shard_map/reduce_scatter | solution.py:175
  117.7 5.9 %gather_fusion = bf16[80,256,128]{2,1,0:T(8,128)(2,1)} fusion(bf16[256,24,128]{2,0,1:T(8,128)(2,1)S(1)} %copy.187, s32[1024]{0:T(1024)} %pad_clamp_fusion.1), kind=kCustom, calls=%fused_computation.clone | custom fusion | bytes 10486080 | tf_op jit(solution)/shard_map/jit(_take)/gather | solution.py:138
  123.6 6.5 %bitcast_multiply_fusion.2 = f32[256,80,128]{2,0,1:T(8,128)S(1)} fusion(f32[256,80]{0,1:T(8,128)S(1)} %copy-done.19, bf16[80,256,128]{2,1,0:T(8,128)(2,1)} %gather_fusion, pred[80]{0:T(512)(128)(4,1)S(1)} %copy-done.37, s32[80,128,128]{2,1,0:T(8,128)} %param.38), kind=kOutput, calls=%fused_computation.8 | convolution fusion | flops 677642240 | bytes 21053520 | tf_op jit(solution)/shard_map/ctj,tjk->ctk/dot_general | solution.py:139
  130.2 9.4 %fusion.78 = bf16[256,8,128]{2,1,0:T(8,128)(2,1)S(1)} fusion(f32[256,8,128]{2,1,0:T(8,128)S(1)} %get-tuple-element.12, f32[8,256,128]{2,0,1:T(8,128)S(1)} %copy-done.15, f32[256,80,128]{2,0,1:T(8,128)S(1)} %bitcast_multiply_fusion.2, s32[80]{0:T(128)S(1)} %copy-done.43), kind=kOutput, calls=%fused_computation.76 | convolution fusion | flops 252445312 | bytes 13107520 | tf_op jit(solution)/shard_map/ctk,tb->cbk/dot_general | solution.py:143
  143.8 2.1 gather_fusion.4
  146.0 4.4 multiply_bitcast_fusion.1
  150.3 3.5 copy.233
  153.9 3.2 fusion.170
  159.2 2.1 copy.193
  161.3 1.3 collective-permute-start.3
  162.6 5.4 %collective-permute-start.2 = (bf16[256,1024]{0,1:T(8,128)(2,1)}, bf16[256,1024]{0,1:T(8,128)(2,1)}, u32[]{:S(2)}, u32[]{:S(2)}) collective-permute-start(bf16[256,1024]{0,1:T(8,128)(2,1)} %copy.193), channel_id=1, source_target_pairs={{0,4},{4,8},{8,12},{12,16},{16,20},{20,24},{24,28},{1,5},{5,9},{9,... | collective-permute-start | bytes 1572872 | tf_op jit(solution)/shard_map/ppermute | solution.py:39
  167.9 52.5 %reduce-scatter.6.cloned.1.call-done = f32[16,256]{1,0:T(8,128)} async-done(((f32[128,256]{1,0:T(8,128)}), f32[16,256]{1,0:T(8,128)}) %reduce-scatter.6.cloned.1.call-update) | async-done | bytes 16400 | tf_op jit(solution)/shard_map/reduce_scatter | solution.py:175
  220.5 1.3 convert_element_type.125
  221.8 1.4 reshape.450
  224.3 1.4 add_convert_fusion.5
  226.5 1.4 collective-permute-start.4
  227.9 3.3 collective-permute-start.5
  235.2 4.7 %collective-permute-start.14 = (bf16[16,256]{1,0:T(8,128)(2,1)}, bf16[16,256]{1,0:T(8,128)(2,1)S(1)}, u32[]{:S(2)}, u32[]{:S(2)}) collective-permute-start(bf16[16,256]{1,0:T(8,128)(2,1)} %reshape.452), channel_id=1, source_target_pairs={{0,28},{4,0},{8,4},{12,8},{16,12},{20,16},{24,20},{28,24},{1,29},{... | collective-permute-start | bytes 24584 | tf_op jit(solution)/shard_map/ppermute | solution.py:24
  239.9 1.3 bitcast_dynamic-update-slice_fusion.13
  241.2 1.3 bitcast_dynamic-update-slice_fusion.12
  242.5 4.7 %collective-permute-start.7 = (bf16[16,256]{1,0:T(8,128)(2,1)}, bf16[16,256]{1,0:T(8,128)(2,1)S(1)}, u32[]{:S(2)}, u32[]{:S(2)}) collective-permute-start(bf16[16,256]{1,0:T(8,128)(2,1)} %collective-permute-done.5), channel_id=1, source_target_pairs={{0,28},{4,0},{8,4},{12,8},{16,12},{20,16},{24,20},{28,24},{1,29},{... | collective-permute-start | bytes 24584 | tf_op jit(solution)/shard_map/ppermute | solution.py:24
  248.4 4.7 %collective-permute-start.16 = (bf16[16,256]{1,0:T(8,128)(2,1)S(1)}, bf16[16,256]{1,0:T(8,128)(2,1)S(1)}, u32[]{:S(2)}, u32[]{:S(2)}) collective-permute-start(bf16[16,256]{1,0:T(8,128)(2,1)S(1)} %collective-permute-done.14), channel_id=1, source_target_pairs={{0,28},{4,0},{8,4},{12,8},{16,12},{20,16},{24,20},{28,24},{1,29},{... | collective-permute-start | bytes 24584 | tf_op jit(solution)/shard_map/ppermute | solution.py:24
  254.3 4.7 %collective-permute-start.9 = (bf16[16,256]{1,0:T(8,128)(2,1)S(1)}, bf16[16,256]{1,0:T(8,128)(2,1)S(1)}, u32[]{:S(2)}, u32[]{:S(2)}) collective-permute-start(bf16[16,256]{1,0:T(8,128)(2,1)S(1)} %collective-permute-done.7), channel_id=1, source_target_pairs={{0,28},{4,0},{8,4},{12,8},{16,12},{20,16},{24,20},{28,24},{1,29},{... | collective-permute-start | bytes 24584 | tf_op jit(solution)/shard_map/ppermute | solution.py:24
  260.2 4.7 %collective-permute-start.18 = (bf16[16,256]{1,0:T(8,128)(2,1)S(1)}, bf16[16,256]{1,0:T(8,128)(2,1)S(1)}, u32[]{:S(2)}, u32[]{:S(2)}) collective-permute-start(bf16[16,256]{1,0:T(8,128)(2,1)S(1)} %collective-permute-done.16), channel_id=1, source_target_pairs={{0,28},{4,0},{8,4},{12,8},{16,12},{20,16},{24,20},{28,24},{1,29},{... | collective-permute-start | bytes 24584 | tf_op jit(solution)/shard_map/ppermute | solution.py:24
  267.8 4.6 %collective-permute-done.10 = bf16[16,256]{1,0:T(8,128)(2,1)S(1)} collective-permute-done((bf16[16,256]{1,0:T(8,128)(2,1)S(1)}, bf16[16,256]{1,0:T(8,128)(2,1)S(1)}, u32[]{:S(2)}, u32[]{:S(2)}) %collective-permute-start.10) | collective-permute-done | bytes 8224 | tf_op jit(solution)/shard_map/ppermute | solution.py:19
  272.9 1.6 copy.205
  275.1 1.6 copy.220
  276.6 1.8 bitcast_multiply_fusion.4
  278.5 3.8 fusion.26
  282.3 2.4 bitcast_multiply_fusion.3
  284.7 2.1 copy.197
  286.8 2.1 copy.195
  288.8 1.4 pad_maximum_fusion.1
  290.2 5.9 %gather_fusion.1 = bf16[80,256,128]{2,1,0:T(8,128)(2,1)} fusion(bf16[256,24,128]{2,0,1:T(8,128)(2,1)S(1)} %pad_maximum_fusion.1, s32[1024]{0:T(1024)} %pad_clamp_fusion.1), kind=kCustom, calls=%fused_computation.2.clone | custom fusion | bytes 10486080 | tf_op jit(solution)/shard_map/jit(_take)/gather | solution.py:138
  296.2 6.5 %bitcast_multiply_fusion.1 = f32[256,80,128]{2,0,1:T(8,128)S(1)} fusion(f32[256,80]{0,1:T(8,128)S(1)} %copy-done.18, bf16[80,256,128]{2,1,0:T(8,128)(2,1)} %gather_fusion.1, pred[80]{0:T(512)(128)(4,1)S(1)} %copy-done.38, s32[80,128,128]{2,1,0:T(8,128)} %param.38), kind=kOutput, calls=%fused_computation.7 | convolution fusion | flops 677642240 | bytes 21053520 | tf_op jit(solution)/shard_map/ctj,tjk->ctk/dot_general | solution.py:139
  302.7 9.4 %fusion.81 = bf16[256,8,128]{2,1,0:T(8,128)(2,1)S(1)} fusion(f32[256,8,128]{2,1,0:T(8,128)S(1)} %get-tuple-element.12, f32[8,256,128]{2,0,1:T(8,128)S(1)} %copy-done.17, f32[256,80,128]{2,0,1:T(8,128)S(1)} %bitcast_multiply_fusion.1, s32[80]{0:T(128)S(1)} %copy-done.44), kind=kOutput, calls=%fused_computation.77 | convolution fusion | flops 252445312 | bytes 13107520 | tf_op jit(solution)/shard_map/ctk,tb->cbk/dot_general | solution.py:143
  313.8 1.4 add_convert_fusion.1
  316.0 2.1 gather_fusion.5
  318.1 4.2 multiply_bitcast_fusion
  322.4 3.6 copy.237
  325.9 3.2 fusion.168
  329.8 5.7 %fusion.24 = f32[8,256,128]{2,0,1:T(8,128)} fusion(f32[256,24,128]{2,0,1:T(8,128)} %bitcast_multiply_fusion.3, s32[24]{0:T(128)S(1)} %copy-done.48), kind=kOutput, calls=%fused_computation.30 | convolution fusion | flops 75497664 | bytes 4194400 | tf_op jit(solution)/shard_map/ctk,tb->cbk/dot_general | solution.py:154
  335.7 1.3 collective-permute-start.12
  337.0 4.6 %collective-permute-start.11 = (bf16[256,1024]{0,1:T(8,128)(2,1)S(1)}, bf16[256,1024]{0,1:T(8,128)(2,1)S(1)}, u32[]{:S(2)}, u32[]{:S(2)}) collective-permute-start(bf16[256,1024]{0,1:T(8,128)(2,1)S(1)} %copy.208), channel_id=1, source_target_pairs={{0,4},{4,8},{8,12},{12,16},{16,20},{20,24},{24,28},{1,5},{5,9},{9,... | collective-permute-start | bytes 1572872 | tf_op jit(solution)/shard_map/ppermute | solution.py:39
  341.6 49.7 %reduce-scatter.8.cloned.1.call-done = f32[16,256]{1,0:T(8,128)} async-done(((f32[128,256]{1,0:T(8,128)}), f32[16,256]{1,0:T(8,128)}) %reduce-scatter.8.cloned.1.call-update) | async-done | bytes 16400 | tf_op jit(solution)/shard_map/reduce_scatter | solution.py:175
  394.6 1.4 pad_maximum_fusion.2
  396.0 5.8 %gather_fusion.3 = bf16[80,256,128]{2,1,0:T(8,128)(2,1)} fusion(bf16[256,24,128]{2,0,1:T(8,128)(2,1)S(1)} %pad_maximum_fusion.2, s32[1024]{0:T(1024)} %pad_clamp_fusion.1), kind=kCustom, calls=%fused_computation.3.clone | custom fusion | bytes 10486080 | tf_op jit(solution)/shard_map/jit(_take)/gather | solution.py:138
  401.7 6.6 %bitcast_multiply_fusion = f32[256,80,128]{2,0,1:T(8,128)S(1)} fusion(f32[256,80]{0,1:T(8,128)S(1)} %copy.213, bf16[80,256,128]{2,1,0:T(8,128)(2,1)} %gather_fusion.3, pred[80]{0:T(512)(128)(4,1)S(1)} %copy-done.38, s32[80,128,128]{2,1,0:T(8,128)} %param.38), kind=kOutput, calls=%fused_computation.6 | convolution fusion | flops 677642240 | bytes 21053520 | tf_op jit(solution)/shard_map/ctj,tjk->ctk/dot_general | solution.py:139
  408.4 9.4 %fusion.84 = bf16[256,8,128]{2,1,0:T(8,128)(2,1)S(1)} fusion(f32[256,8,128]{2,1,0:T(8,128)S(1)} %get-tuple-element.12, f32[8,256,128]{2,0,1:T(8,128)S(1)} %copy-done.16, f32[256,80,128]{2,0,1:T(8,128)S(1)} %bitcast_multiply_fusion, s32[80]{0:T(128)S(1)} %copy-done.45), kind=kOutput, calls=%fused_computation.78 | convolution fusion | flops 252445312 | bytes 13107520 | tf_op jit(solution)/shard_map/ctk,tb->cbk/dot_general | solution.py:143
  419.9 1.6 reshape.553
  421.5 3.5 all-to-all-start
  426.1 7.6 %all-to-all-done = bf16[4,2,32768]{2,1,0:T(2,128)(2,1)S(1)} async-done(((bf16[4,2,32768]{2,1,0:T(2,128)(2,1)}), bf16[4,2,32768]{2,1,0:T(2,128)(2,1)S(1)}, u32[]{:S(2)}, u32[]{:S(2)}) %all-to-all-start) | async-done | bytes 524320 | tf_op jit(solution)/shard_map/all_to_all | solution.py:196
  (284 shorter events, 63.6 us)
Async XLA Ops:
  7.2 105.3 %reduce-scatter.4.cloned.1.call-start = ((), (), s32[]{:S(2)}) async-start(), calls=%async_computation.4 | async-start | bytes 147456 | tf_op jit(solution)/shard_map/reduce_scatter | solution.py:175
  12.1 102.7 %collective-permute-start.1 = (bf16[256,1024]{1,0:T(8,128)(2,1)}, bf16[256,1024]{1,0:T(8,128)(2,1)}, u32[]{:S(2)}, u32[]{:S(2)}) collective-permute-start(bf16[256,1024]{1,0:T(8,128)(2,1)} %fusion.90), channel_id=1, source_target_pairs={{4,0},{8,4},{12,8},{16,12},{20,16},{24,20},{28,24},{5,1},{9,5},{13... | collective-permute-start | bytes 1572872 | tf_op jit(solution)/shard_map/ppermute | solution.py:41
  13.3 102.5 %collective-permute-start = (bf16[256,1024]{1,0:T(8,128)(2,1)}, bf16[256,1024]{1,0:T(8,128)(2,1)}, u32[]{:S(2)}, u32[]{:S(2)}) collective-permute-start(bf16[256,1024]{1,0:T(8,128)(2,1)} %fusion.90), channel_id=1, source_target_pairs={{0,4},{4,8},{8,12},{12,16},{16,20},{20,24},{24,28},{1,5},{5,9},{9,... | collective-permute-start | bytes 1572872 | tf_op jit(solution)/shard_map/ppermute | solution.py:39
  27.4 4.0 copy-start.35
  33.7 4.3 copy-start.6
  45.6 4.4 %copy-start.62 = (s32[24,2]{0,1:T(2,128)S(1)}, s32[24,2]{0,1:T(2,128)}, u32[]{:S(2)}) copy-start(s32[24,2]{0,1:T(2,128)} %param.42) | copy-start | bytes 580
  45.6 5.0 %copy-start.63 = (s32[80]{0:T(128)S(1)}, s32[80]{0:T(128)}, u32[]{:S(2)}) copy-start(s32[80]{0:T(128)} %param.37) | copy-start | bytes 964
  45.6 8.5 %copy-start.57 = (f32[3,64]{1,0:T(4,128)S(1)}, f32[3,64]{1,0:T(4,128)}, u32[]{:S(2)}) copy-start(f32[3,64]{1,0:T(4,128)} %param.33) | copy-start | bytes 2308
  45.6 9.1 %copy-start.61 = (s32[80,2]{0,1:T(2,128)S(1)}, s32[80,2]{0,1:T(2,128)}, u32[]{:S(2)}) copy-start(s32[80,2]{0,1:T(2,128)} %param.36) | copy-start | bytes 1924
  45.6 9.6 %copy-start.4 = (s32[24,128,128]{2,1,0:T(8,128)S(1)}, s32[24,128,128]{2,1,0:T(8,128)}, u32[]{:S(2)}) copy-start(s32[24,128,128]{2,1,0:T(8,128)} %param.44) | copy-start | bytes 4718596
  49.5 171.0 %reduce-scatter.6.cloned.1.call-start = ((), (), s32[]{:S(2)}) async-start(), calls=%async_computation.5 | async-start | bytes 147456 | tf_op jit(solution)/shard_map/reduce_scatter | solution.py:175
  50.6 9.8 %copy-start.46 = (s32[24]{0:T(128)}, s32[24]{0:T(128)S(1)}, u32[]{:S(2)}) copy-start(s32[24]{0:T(128)S(1)} %subtract_bitcast_fusion) | copy-start | bytes 292
  54.7 58.6 %copy-start.50 = (f32[64]{0:T(128)}, f32[64]{0:T(128)S(1)}, u32[]{:S(2)}) copy-start(f32[64]{0:T(128)S(1)} %get-tuple-element.22) | copy-start | bytes 772
  56.4 3.9 copy-start.58
  56.4 3.9 copy-start.59
  56.4 4.5 %copy-start.26 = (bf16[128,64]{0,1:T(8,128)(2,1)S(1)}, bf16[128,64]{0,1:T(8,128)(2,1)}, u32[]{:S(2)}) copy-start(bf16[128,64]{0,1:T(8,128)(2,1)} %param.45) | copy-start | bytes 49156
  56.4 4.5 %copy-start.34 = (f32[16,64]{1,0:T(8,128)S(1)}, f32[16,64]{1,0:T(8,128)}, u32[]{:S(2)}) copy-start(f32[16,64]{1,0:T(8,128)} %copy-done.33) | copy-start | bytes 12292
  56.5 4.5 %copy-start.60 = (f32[64]{0:T(128)S(1)}, f32[64]{0:T(128)}, u32[]{:S(2)}) copy-start(f32[64]{0:T(128)} %param.46) | copy-start | bytes 772
  56.5 60.5 %copy-start.14 = (bf16[256,8,128]{2,1,0:T(8,128)(2,1)S(1)}, bf16[256,8,128]{2,1,0:T(8,128)(2,1)}, u32[]{:S(2)}) copy-start(bf16[256,8,128]{2,1,0:T(8,128)(2,1)} %copy-done.13) | copy-start | bytes 1572868
  61.2 51.3 %copy-start.29 = (f32[16,64]{1,0:T(8,128)}, f32[16,64]{1,0:T(8,128)S(1)}, u32[]{:S(2)}) copy-start(f32[16,64]{1,0:T(8,128)S(1)} %convolution_add_fusion.8) | copy-start | bytes 12292
  117.6 5.9 %copy-start.19 = (f32[256,80]{0,1:T(8,128)S(1)}, f32[256,80]{0,1:T(8,128)}, u32[]{:S(2)}) copy-start(f32[256,80]{0,1:T(8,128)} %copy.188) | copy-start | bytes 245764
  117.7 5.9 %copy-start.37 = (pred[80]{0:T(512)(128)(4,1)S(1)}, pred[80]{0:T(512)(128)(4,1)}, u32[]{:S(2)}) copy-start(pred[80]{0:T(512)(128)(4,1)} %get-tuple-element.9) | copy-start | bytes 244
  123.6 6.6 %copy-start.15 = (f32[8,256,128]{2,0,1:T(8,128)S(1)}, f32[8,256,128]{2,0,1:T(8,128)}, u32[]{:S(2)}) copy-start(f32[8,256,128]{2,0,1:T(8,128)} %fusion.28) | copy-start | bytes 3145732
  123.6 6.6 %copy-start.43 = (s32[80]{0:T(128)S(1)}, s32[80]{0:T(128)}, u32[]{:S(2)}) copy-start(s32[80]{0:T(128)} %subtract_bitcast_fusion.1) | copy-start | bytes 964
  130.2 9.6 %copy-start.51 = (f32[64]{0:T(128)S(1)}, f32[64]{0:T(128)}, u32[]{:S(2)}) copy-start(f32[64]{0:T(128)} %copy-done.50) | copy-start | bytes 772
  141.8 4.1 copy-start.7
  153.9 122.8 %copy-start.5 = (s32[24,128,128]{2,1,0:T(8,128)S(1)}, s32[24,128,128]{2,1,0:T(8,128)}, u32[]{:S(2)}) copy-start(s32[24,128,128]{2,1,0:T(8,128)} %param.44) | copy-start | bytes 4718596
  157.8 233.5 %reduce-scatter.8.cloned.1.call-start = ((), (), s32[]{:S(2)}) async-start(), calls=%async_computation.6 | async-start | bytes 147456 | tf_op jit(solution)/shard_map/reduce_scatter | solution.py:175
  161.3 123.4 %collective-permute-start.3 = (bf16[256,1024]{0,1:T(8,128)(2,1)}, bf16[256,1024]{0,1:T(8,128)(2,1)}, u32[]{:S(2)}, u32[]{:S(2)}) collective-permute-start(bf16[256,1024]{0,1:T(8,128)(2,1)} %copy.193), channel_id=1, source_target_pairs={{4,0},{8,4},{12,8},{16,12},{20,16},{24,20},{28,24},{5,1},{9,5},{13... | collective-permute-start | bytes 1572872 | tf_op jit(solution)/shard_map/ppermute | solution.py:41
  162.6 124.2 %collective-permute-start.2 = (bf16[256,1024]{0,1:T(8,128)(2,1)}, bf16[256,1024]{0,1:T(8,128)(2,1)}, u32[]{:S(2)}, u32[]{:S(2)}) collective-permute-start(bf16[256,1024]{0,1:T(8,128)(2,1)} %copy.193), channel_id=1, source_target_pairs={{0,4},{4,8},{8,12},{12,16},{16,20},{20,24},{24,28},{1,5},{5,9},{9,... | collective-permute-start | bytes 1572872 | tf_op jit(solution)/shard_map/ppermute | solution.py:39
  226.5 8.7 %collective-permute-start.4 = (bf16[16,256]{1,0:T(8,128)(2,1)}, bf16[16,256]{1,0:T(8,128)(2,1)}, u32[]{:S(2)}, u32[]{:S(2)}) collective-permute-start(bf16[16,256]{1,0:T(8,128)(2,1)} %reshape.441), channel_id=1, source_target_pairs={{0,4},{4,8},{8,12},{12,16},{16,20},{20,24},{24,28},{28,0},{1,5},{5... | collective-permute-start | bytes 24584 | tf_op jit(solution)/shard_map/ppermute | solution.py:19
  227.9 13.2 %collective-permute-start.5 = (bf16[16,256]{1,0:T(8,128)(2,1)}, bf16[16,256]{1,0:T(8,128)(2,1)}, u32[]{:S(2)}, u32[]{:S(2)}) collective-permute-start(bf16[16,256]{1,0:T(8,128)(2,1)} %reshape.441), channel_id=1, source_target_pairs={{0,28},{4,0},{8,4},{12,8},{16,12},{20,16},{24,20},{28,24},{1,29},{... | collective-permute-start | bytes 24584 | tf_op jit(solution)/shard_map/ppermute | solution.py:24
  232.7 9.8 %collective-permute-start.13 = (bf16[16,256]{1,0:T(8,128)(2,1)}, bf16[16,256]{1,0:T(8,128)(2,1)S(1)}, u32[]{:S(2)}, u32[]{:S(2)}) collective-permute-start(bf16[16,256]{1,0:T(8,128)(2,1)} %reshape.452), channel_id=1, source_target_pairs={{0,4},{4,8},{8,12},{12,16},{16,20},{20,24},{24,28},{28,0},{1,5},{5... | collective-permute-start | bytes 24584 | tf_op jit(solution)/shard_map/ppermute | solution.py:19
  233.9 44.5 %copy-start.47 = (s32[24]{0:T(128)S(1)}, s32[24]{0:T(128)}, u32[]{:S(2)}) copy-start(s32[24]{0:T(128)} %copy-done.46) | copy-start | bytes 292
  235.2 12.6 %collective-permute-start.14 = (bf16[16,256]{1,0:T(8,128)(2,1)}, bf16[16,256]{1,0:T(8,128)(2,1)S(1)}, u32[]{:S(2)}, u32[]{:S(2)}) collective-permute-start(bf16[16,256]{1,0:T(8,128)(2,1)} %reshape.452), channel_id=1, source_target_pairs={{0,28},{4,0},{8,4},{12,8},{16,12},{20,16},{24,20},{28,24},{1,29},{... | collective-permute-start | bytes 24584 | tf_op jit(solution)/shard_map/ppermute | solution.py:24
  241.2 7.2 %collective-permute-start.6 = (bf16[16,256]{1,0:T(8,128)(2,1)}, bf16[16,256]{1,0:T(8,128)(2,1)S(1)}, u32[]{:S(2)}, u32[]{:S(2)}) collective-permute-start(bf16[16,256]{1,0:T(8,128)(2,1)} %collective-permute-done.4), channel_id=1, source_target_pairs={{0,4},{4,8},{8,12},{12,16},{16,20},{20,24},{24,28},{28,0},{1,5},{5... | collective-permute-start | bytes 24584 | tf_op jit(solution)/shard_map/ppermute | solution.py:19
  242.5 11.2 %collective-permute-start.7 = (bf16[16,256]{1,0:T(8,128)(2,1)}, bf16[16,256]{1,0:T(8,128)(2,1)S(1)}, u32[]{:S(2)}, u32[]{:S(2)}) collective-permute-start(bf16[16,256]{1,0:T(8,128)(2,1)} %collective-permute-done.5), channel_id=1, source_target_pairs={{0,28},{4,0},{8,4},{12,8},{16,12},{20,16},{24,20},{28,24},{1,29},{... | collective-permute-start | bytes 24584 | tf_op jit(solution)/shard_map/ppermute | solution.py:24
  247.8 6.5 %collective-permute-start.15 = (bf16[16,256]{1,0:T(8,128)(2,1)S(1)}, bf16[16,256]{1,0:T(8,128)(2,1)S(1)}, u32[]{:S(2)}, u32[]{:S(2)}) collective-permute-start(bf16[16,256]{1,0:T(8,128)(2,1)S(1)} %collective-permute-done.13), channel_id=1, source_target_pairs={{0,4},{4,8},{8,12},{12,16},{16,20},{20,24},{24,28},{28,0},{1,5},{5... | collective-permute-start | bytes 24584 | tf_op jit(solution)/shard_map/ppermute | solution.py:19
  248.4 11.3 %collective-permute-start.16 = (bf16[16,256]{1,0:T(8,128)(2,1)S(1)}, bf16[16,256]{1,0:T(8,128)(2,1)S(1)}, u32[]{:S(2)}, u32[]{:S(2)}) collective-permute-start(bf16[16,256]{1,0:T(8,128)(2,1)S(1)} %collective-permute-done.14), channel_id=1, source_target_pairs={{0,28},{4,0},{8,4},{12,8},{16,12},{20,16},{24,20},{28,24},{1,29},{... | collective-permute-start | bytes 24584 | tf_op jit(solution)/shard_map/ppermute | solution.py:24
  253.7 6.5 %collective-permute-start.8 = (bf16[16,256]{1,0:T(8,128)(2,1)S(1)}, bf16[16,256]{1,0:T(8,128)(2,1)S(1)}, u32[]{:S(2)}, u32[]{:S(2)}) collective-permute-start(bf16[16,256]{1,0:T(8,128)(2,1)S(1)} %collective-permute-done.6), channel_id=1, source_target_pairs={{0,4},{4,8},{8,12},{12,16},{16,20},{20,24},{24,28},{28,0},{1,5},{5... | collective-permute-start | bytes 24584 | tf_op jit(solution)/shard_map/ppermute | solution.py:19
  254.3 12.3 %collective-permute-start.9 = (bf16[16,256]{1,0:T(8,128)(2,1)S(1)}, bf16[16,256]{1,0:T(8,128)(2,1)S(1)}, u32[]{:S(2)}, u32[]{:S(2)}) collective-permute-start(bf16[16,256]{1,0:T(8,128)(2,1)S(1)} %collective-permute-done.7), channel_id=1, source_target_pairs={{0,28},{4,0},{8,4},{12,8},{16,12},{20,16},{24,20},{28,24},{1,29},{... | collective-permute-start | bytes 24584 | tf_op jit(solution)/shard_map/ppermute | solution.py:24
  259.6 6.3 %collective-permute-start.17 = (bf16[16,256]{1,0:T(8,128)(2,1)S(1)}, bf16[16,256]{1,0:T(8,128)(2,1)S(1)}, u32[]{:S(2)}, u32[]{:S(2)}) collective-permute-start(bf16[16,256]{1,0:T(8,128)(2,1)S(1)} %collective-permute-done.15), channel_id=1, source_target_pairs={{0,4},{4,8},{8,12},{12,16},{16,20},{20,24},{24,28},{28,0},{1,5},{5... | collective-permute-start | bytes 24584 | tf_op jit(solution)/shard_map/ppermute | solution.py:19
  260.2 6.9 %collective-permute-start.18 = (bf16[16,256]{1,0:T(8,128)(2,1)S(1)}, bf16[16,256]{1,0:T(8,128)(2,1)S(1)}, u32[]{:S(2)}, u32[]{:S(2)}) collective-permute-start(bf16[16,256]{1,0:T(8,128)(2,1)S(1)} %collective-permute-done.16), channel_id=1, source_target_pairs={{0,28},{4,0},{8,4},{12,8},{16,12},{20,16},{24,20},{28,24},{1,29},{... | collective-permute-start | bytes 24584 | tf_op jit(solution)/shard_map/ppermute | solution.py:24
  266.0 6.3 %collective-permute-start.10 = (bf16[16,256]{1,0:T(8,128)(2,1)S(1)}, bf16[16,256]{1,0:T(8,128)(2,1)S(1)}, u32[]{:S(2)}, u32[]{:S(2)}) collective-permute-start(bf16[16,256]{1,0:T(8,128)(2,1)S(1)} %collective-permute-done.8), channel_id=1, source_target_pairs={{0,4},{4,8},{8,12},{12,16},{16,20},{20,24},{24,28},{28,0},{1,5},{5... | collective-permute-start | bytes 24584 | tf_op jit(solution)/shard_map/ppermute | solution.py:19
  266.6 7.9 %collective-permute-start.19 = (bf16[16,256]{1,0:T(8,128)(2,1)S(1)}, bf16[16,256]{1,0:T(8,128)(2,1)S(1)}, u32[]{:S(2)}, u32[]{:S(2)}) collective-permute-start(bf16[16,256]{1,0:T(8,128)(2,1)S(1)} %collective-permute-done.17), channel_id=1, source_target_pairs={{0,4},{4,8},{8,12},{12,16},{16,20},{20,24},{24,28},{28,0},{1,5},{5... | collective-permute-start | bytes 24584 | tf_op jit(solution)/shard_map/ppermute | solution.py:19
  290.2 5.9 %copy-start.18 = (f32[256,80]{0,1:T(8,128)S(1)}, f32[256,80]{0,1:T(8,128)}, u32[]{:S(2)}) copy-start(f32[256,80]{0,1:T(8,128)} %copy.198) | copy-start | bytes 245764
  290.2 5.9 %copy-start.38 = (pred[80]{0:T(512)(128)(4,1)S(1)}, pred[80]{0:T(512)(128)(4,1)}, u32[]{:S(2)}) copy-start(pred[80]{0:T(512)(128)(4,1)} %get-tuple-element.9) | copy-start | bytes 244
  296.1 6.6 %copy-start.17 = (f32[8,256,128]{2,0,1:T(8,128)S(1)}, f32[8,256,128]{2,0,1:T(8,128)}, u32[]{:S(2)}) copy-start(f32[8,256,128]{2,0,1:T(8,128)} %fusion.26) | copy-start | bytes 3145732
  296.1 6.6 %copy-start.44 = (s32[80]{0:T(128)S(1)}, s32[80]{0:T(128)}, u32[]{:S(2)}) copy-start(s32[80]{0:T(128)} %subtract_bitcast_fusion.1) | copy-start | bytes 964
  325.9 3.9 copy-start.48
  325.9 9.5 %copy-start.10 = (bf16[4,64,1024]{2,1,0:T(8,128)(2,1)S(1)}, bf16[4,64,1024]{2,1,0:T(8,128)(2,1)}, u32[]{:S(2)}) copy-start(bf16[4,64,1024]{2,1,0:T(8,128)(2,1)} %copy-done.9) | copy-start | bytes 1572868
  329.1 63.0 %copy-start.21 = (bf16[3,64,64]{2,1,0:T(8,128)(2,1)S(1)}, bf16[3,64,64]{2,1,0:T(8,128)(2,1)}, u32[]{:S(2)}) copy-start(bf16[3,64,64]{2,1,0:T(8,128)(2,1)} %param.32) | copy-start | bytes 73732
  329.1 63.0 %copy-start.49 = (f32[64]{0:T(128)S(1)}, f32[64]{0:T(128)}, u32[]{:S(2)}) copy-start(f32[64]{0:T(128)} %get-tuple-element.21) | copy-start | bytes 772
  335.7 56.8 %collective-permute-start.12 = (bf16[256,1024]{0,1:T(8,128)(2,1)S(1)}, bf16[256,1024]{0,1:T(8,128)(2,1)S(1)}, u32[]{:S(2)}, u32[]{:S(2)}) collective-permute-start(bf16[256,1024]{0,1:T(8,128)(2,1)S(1)} %copy.208), channel_id=1, source_target_pairs={{4,0},{8,4},{12,8},{16,12},{20,16},{24,20},{28,24},{5,1},{9,5},{13... | collective-permute-start | bytes 1572872 | tf_op jit(solution)/shard_map/ppermute | solution.py:41
  337.0 56.6 %collective-permute-start.11 = (bf16[256,1024]{0,1:T(8,128)(2,1)S(1)}, bf16[256,1024]{0,1:T(8,128)(2,1)S(1)}, u32[]{:S(2)}, u32[]{:S(2)}) collective-permute-start(bf16[256,1024]{0,1:T(8,128)(2,1)S(1)} %copy.208), channel_id=1, source_target_pairs={{0,4},{4,8},{8,12},{12,16},{16,20},{20,24},{24,28},{1,5},{5,9},{9,... | collective-permute-start | bytes 1572872 | tf_op jit(solution)/shard_map/ppermute | solution.py:39
  401.7 6.6 %copy-start.16 = (f32[8,256,128]{2,0,1:T(8,128)S(1)}, f32[8,256,128]{2,0,1:T(8,128)}, u32[]{:S(2)}) copy-start(f32[8,256,128]{2,0,1:T(8,128)} %fusion.24) | copy-start | bytes 3145732
  401.7 6.6 %copy-start.45 = (s32[80]{0:T(128)S(1)}, s32[80]{0:T(128)}, u32[]{:S(2)}) copy-start(s32[80]{0:T(128)} %subtract_bitcast_fusion.1) | copy-start | bytes 964
  418.8 6.1 %copy-start.27 = (bf16[128,64]{0,1:T(8,128)(2,1)S(1)}, bf16[128,64]{0,1:T(8,128)(2,1)}, u32[]{:S(2)}) copy-start(bf16[128,64]{0,1:T(8,128)(2,1)} %param.45) | copy-start | bytes 49156
  418.8 6.2 %copy-start.28 = (bf16[16,4,64]{2,0,1:T(8,128)(2,1)S(1)}, bf16[16,4,64]{2,0,1:T(8,128)(2,1)}, u32[]{:S(2)}) copy-start(bf16[16,4,64]{2,0,1:T(8,128)(2,1)} %get-tuple-element.4) | copy-start | bytes 24580
  418.8 6.2 %copy-start.54 = (f32[4,64]{1,0:T(4,128)S(1)}, f32[4,64]{1,0:T(4,128)}, u32[]{:S(2)}) copy-start(f32[4,64]{1,0:T(4,128)} %constant_dynamic-slice_fusion) | copy-start | bytes 3076
  418.8 6.4 %copy-start.52 = (f32[64]{0:T(128)S(1)}, f32[64]{0:T(128)}, u32[]{:S(2)}) copy-start(f32[64]{0:T(128)} %param.47) | copy-start | bytes 772
  419.9 15.1 %copy-start.30 = (f32[16,64]{1,0:T(8,128)S(1)}, f32[16,64]{1,0:T(8,128)}, u32[]{:S(2)}) copy-start(f32[16,64]{1,0:T(8,128)} %copy-done.29) | copy-start | bytes 12292
  421.5 12.3 %all-to-all-start = ((bf16[4,2,32768]{2,1,0:T(2,128)(2,1)}), bf16[4,2,32768]{2,1,0:T(2,128)(2,1)S(1)}, u32[]{:S(2)}, u32[]{:S(2)}) async-start(bf16[4,2,32768]{2,1,0:T(2,128)(2,1)} %reshape.553), calls=%async_computation.2 | async-start | bytes 1048576 | tf_op jit(solution)/shard_map/all_to_all | solution.py:196
  425.0 11.6 %copy-start.1 = (bf16[822,64]{0,1:T(8,128)(2,1)S(1)}, bf16[822,64]{0,1:T(8,128)(2,1)}, u32[]{:S(2)}) copy-start(bf16[822,64]{0,1:T(8,128)(2,1)} %param.30) | copy-start | bytes 315652
  (24 other events, 45.5 us)
Sparse Core Ops, SparseCore 0:
  49.6 62.7 reduce-scatter.3
  157.9 62.5 reduce-scatter.5
  329.9 61.3 reduce-scatter.7
